TPU v7x, 256 devices: a whole 4x4x8 slice. The times are simulated.
256 devices in a mesh: chan: 32 (over x, z), win: 8 (over y, core).
Axes of the slice: x: 4, y: 4, z: 8, core: 2. Of those that a mesh axis runs over, the one named last changes fastest.
Arguments:
- spectra: bfloat16 [2, 16, 2048, 1024], P(None, 'win', 'chan'), may hold values from -200 to 200
- pair_blocks: int32 [256, 2], P(('chan', 'win')), may hold values from 0 to 31, as said below
Outputs:
- stacks: float32 [256, 64, 64, 256], P(('chan', 'win'))
Inputs may be any that keep to these rules, and one draw needn't show every extreme that they name: `pair_blocks`: row p belongs to channel block c = p // 8. The 8 rows of c hold, in a drawn order and each in a drawn orientation, the pairs of blocks c - d // 2 and c - d // 2 + d for d = 0 to 7, block numbers taken modulo 32; so every pair of blocks at cyclic distance below 8 appears exactly once in all.
All inputs are finite; a program needn't handle non-finite values.
Results may differ from a plain program's by a relative error of at most 0.0032.
Values may be sent and summed in bfloat16 or wider, within the bound.
No kernel may reach another device: no remote copies, remote signals or barrier semaphores. Data moves between devices by JAX's collectives and lax.ppermute only.
A program may use at most 256 MiB of HBM per device.

v0:
```python
import math
import jax
import jax.numpy as jnp
from jax import lax
from jax.sharding import PartitionSpec as P

NLAG = 256
HALF_BAND = 64
eps = 1e-05
first_bin = 60.0
samples = 15000.0


def shifted(block, axis, distance):
    devices = range(lax.axis_size(axis))
    route = [((i - distance) % len(devices), i) for i in devices]
    return lax.ppermute(block, axis, route)


def smoothing(length_bins, half_width):
    indices = jnp.arange(length_bins, dtype=jnp.int32)
    return (jnp.abs(indices[:, None] - indices[None, :]) <= half_width).astype(jnp.float32)


def whiten(spectra):
    length_bins = spectra.shape[-1]
    real_part = spectra[0].astype(jnp.float32)
    imag_part = spectra[1].astype(jnp.float32)
    powers = real_part * real_part + imag_part * imag_part
    smoother = smoothing(length_bins, HALF_BAND)
    counts = jnp.sum(smoother, axis=0)
    rows_flat = powers.reshape(-1, length_bins)
    smooth = jnp.dot(rows_flat, smoother, precision=lax.Precision.HIGHEST) / counts
    factor = lax.rsqrt(smooth + eps).reshape(powers.shape)
    return jnp.stack([real_part * factor, imag_part * factor]).astype(jnp.bfloat16)


def make_table(length_bins):
    bin_freq = first_bin + jnp.arange(length_bins, dtype=jnp.float32)
    lag_steps = jnp.arange(NLAG, dtype=jnp.float32) - NLAG // 2
    angles = 2.0 * math.pi / samples * bin_freq[:, None] * lag_steps[None, :]
    return jnp.concatenate([jnp.cos(angles), -jnp.sin(angles)], axis=0).astype(jnp.bfloat16)


def cross_spectrum(leading, trailing):
    left_rows = jnp.concatenate([leading[0], leading[1]], axis=0)
    real_rows = jnp.concatenate([trailing[0], trailing[1]], axis=0)
    imag_rows = jnp.concatenate([-trailing[1], trailing[0]], axis=0)
    real_sum = jnp.einsum("wif,wjf->fij", left_rows, real_rows, preferred_element_type=jnp.float32)
    imag_sum = jnp.einsum("wif,wjf->fij", left_rows, imag_rows, preferred_element_type=jnp.float32)
    return jnp.concatenate([real_sum.astype(jnp.bfloat16), imag_sum.astype(jnp.bfloat16)], axis=0)


def per_device(spectra, pair_blocks):
    whitened = whiten(spectra)
    block_size = spectra.shape[2]
    length_bins = spectra.shape[3]
    centre = lax.axis_index("chan")
    block_count = lax.axis_size("chan")
    reach = pair_blocks.shape[0] * lax.axis_size("win") // 2
    offsets = range(1 - reach, reach + 1)
    gathered = lax.all_gather(whitened, "win", axis=1, tiled=True)
    nearby = jnp.stack(
        [gathered if offset == 0 else shifted(gathered, "chan", -offset) for offset in offsets]
    )
    window_total = nearby.shape[2]
    lag_table = make_table(length_bins)
    scaling = 1.0 / math.sqrt(window_total * length_bins)
    base_block = centre - (reach - 1)

    def correlate(pair_row):
        first_slot = jnp.mod(pair_row[0] - base_block, block_count)
        second_slot = jnp.mod(pair_row[1] - base_block, block_count)
        leading = lax.dynamic_index_in_dim(nearby, first_slot, 0, keepdims=False)
        trailing = lax.dynamic_index_in_dim(nearby, second_slot, 0, keepdims=False)
        cross = cross_spectrum(leading, trailing).reshape(2 * length_bins, block_size * block_size)
        result = lax.dot_general(
            cross, lag_table, (((0,), (0,)), ((), ())), preferred_element_type=jnp.float32
        )
        return result.reshape(block_size, block_size, NLAG) * scaling

    return lax.map(correlate, pair_blocks)


def solution(mesh):
    in_specs = (P(None, "win", "chan", None), P(("chan", "win"), None))
    out_specs = P(("chan", "win"), None, None, None)
    return jax.shard_map(
        per_device, mesh=mesh, in_specs=in_specs, out_specs=out_specs, check_vma=False
    )
```

profile of v0, /device:TPU:6, one launch (start us, length us, event | category | flops | bytes accessed | tf_op | source)
XLA Modules:
  0.0 975.5 jit_solution(2766177840453865730)
XLA Ops:
  11.1 37.7 %all-gather.2.cloned.1.call-done = bf16[2,16,64,1024]{3,2,0,1:T(8,128)(2,1)} async-done(((bf16[2,2,64,1024]{3,2,0,1:T(8,128)(2,1)}), bf16[2,16,64,1024]{3,2,0,1:T(8,128)(2,1)}) %all-gather.2.cloned.1.call-update) | async-done | bytes 4194320 | tf_op jit(solution)/shard_map/all_gather | solution.py:62
  65.1 266.4 %collective-permute-done = bf16[2,16,64,1024]{3,2,1,0:T(8,128)(2,1)} collective-permute-done((bf16[2,16,64,1024]{3,2,1,0:T(8,128)(2,1)}, bf16[2,16,64,1024]{3,2,1,0:T(8,128)(2,1)}, u32[]{:S(2)}, u32[]{:S(2)}) %collective-permute-start) | collective-permute-done | bytes 4194336 | tf_op jit(solution)/shard_map/ppermute | solution.py:17
  341.2 11.0 %copy.38 = bf16[2,16,64,1024]{2,1,3,0:T(8,128)(2,1)} copy(bf16[2,16,64,1024]{3,2,0,1:T(8,128)(2,1)} %all-gather.2.cloned.1.call-done) | data formatting | bytes 8388608 | tf_op jit(solution)/shard_map/all_gather | solution.py:62
  352.2 10.9 %copy.33 = bf16[2,16,64,1024]{2,1,3,0:T(8,128)(2,1)} copy(bf16[2,16,64,1024]{3,2,1,0:T(8,128)(2,1)} %collective-permute-done) | data formatting | bytes 8388608 | tf_op jit(solution)/shard_map/ppermute | solution.py:17
  363.1 148.6 %collective-permute-done.1 = bf16[2,16,64,1024]{3,2,1,0:T(8,128)(2,1)} collective-permute-done((bf16[2,16,64,1024]{3,2,1,0:T(8,128)(2,1)}, bf16[2,16,64,1024]{3,2,1,0:T(8,128)(2,1)}, u32[]{:S(2)}, u32[]{:S(2)}) %collective-permute-start.1) | collective-permute-done | bytes 4194336 | tf_op jit(solution)/shard_map/ppermute | solution.py:17
  516.3 10.9 %copy.35 = bf16[2,16,64,1024]{2,1,3,0:T(8,128)(2,1)} copy(bf16[2,16,64,1024]{3,2,1,0:T(8,128)(2,1)} %collective-permute-done.1) | data formatting | bytes 8388608 | tf_op jit(solution)/shard_map/ppermute | solution.py:17
  527.2 74.2 %collective-permute-done.2 = bf16[2,16,64,1024]{3,2,1,0:T(8,128)(2,1)} collective-permute-done((bf16[2,16,64,1024]{3,2,1,0:T(8,128)(2,1)}, bf16[2,16,64,1024]{3,2,1,0:T(8,128)(2,1)}, u32[]{:S(2)}, u32[]{:S(2)}) %collective-permute-start.2) | collective-permute-done | bytes 4194336 | tf_op jit(solution)/shard_map/ppermute | solution.py:17
  601.4 10.9 %copy.37 = bf16[2,16,64,1024]{2,1,3,0:T(8,128)(2,1)} copy(bf16[2,16,64,1024]{3,2,1,0:T(8,128)(2,1)} %collective-permute-done.2) | data formatting | bytes 8388608 | tf_op jit(solution)/shard_map/ppermute | solution.py:17
  612.3 10.9 %copy.40 = bf16[2,16,64,1024]{2,1,3,0:T(8,128)(2,1)} copy(bf16[2,16,64,1024]{3,2,1,0:T(8,128)(2,1)} %collective-permute-done.3) | data formatting | bytes 8388608 | tf_op jit(solution)/shard_map/ppermute | solution.py:17
  623.3 10.9 %copy.42 = bf16[2,16,64,1024]{2,1,3,0:T(8,128)(2,1)} copy(bf16[2,16,64,1024]{3,2,1,0:T(8,128)(2,1)} %collective-permute-done.4) | data formatting | bytes 8388608 | tf_op jit(solution)/shard_map/ppermute | solution.py:17
  634.2 8.0 bitcast_dynamic-update-slice_fusion.7
  642.2 8.0 bitcast_dynamic-update-slice_fusion.6
  650.2 135.4 %collective-permute-done.5 = bf16[2,16,64,1024]{3,2,1,0:T(8,128)(2,1)} collective-permute-done((bf16[2,16,64,1024]{3,2,1,0:T(8,128)(2,1)}, bf16[2,16,64,1024]{3,2,1,0:T(8,128)(2,1)}, u32[]{:S(2)}, u32[]{:S(2)}) %collective-permute-start.5) | collective-permute-done | bytes 4194336 | tf_op jit(solution)/shard_map/ppermute | solution.py:17
  785.6 11.0 %copy.44 = bf16[2,16,64,1024]{2,1,3,0:T(8,128)(2,1)} copy(bf16[2,16,64,1024]{3,2,1,0:T(8,128)(2,1)} %collective-permute-done.5) | data formatting | bytes 8388608 | tf_op jit(solution)/shard_map/ppermute | solution.py:17
  796.7 8.0 bitcast_dynamic-update-slice_fusion.5
  804.7 8.0 bitcast_dynamic-update-slice_fusion.4
  836.9 10.9 %copy.46 = bf16[2,16,64,1024]{2,1,3,0:T(8,128)(2,1)} copy(bf16[2,16,64,1024]{3,2,1,0:T(8,128)(2,1)} %collective-permute-done.6) | data formatting | bytes 8388608 | tf_op jit(solution)/shard_map/ppermute | solution.py:17
  847.8 8.0 bitcast_dynamic-update-slice_fusion
  860.8 8.8 dynamic-slice_bitcast_fusion.3
  869.7 15.6 %convolution_convert_fusion = bf16[1024,64,64]{2,1,0:T(8,128)(2,1)} fusion(bf16[16,64,1024]{1,0,2:T(8,128)(2,1)} %get-tuple-element.24, bf16[16,64,1024]{1,0,2:T(8,128)(2,1)} %get-tuple-element.15, bf16[16,64,1024]{1,0,2:T(8,128)(2,1)} %get-tuple-element.26, bf16[16,64,1024]{1,0,2:T(8,128)(2,1)} %get-tuple-element.17), kind=kOutput, calls=%fused_computation.3 | convolution fusion | flops 289406976 | bytes 16777216 | tf_op jit(solution)/shard_map/while/body/eval_jaxpr/wif,wjf->fij/dot_general | solution.py:50
  885.3 13.7 %convolution_convert_fusion.1 = bf16[1024,64,64]{2,1,0:T(8,128)(2,1)} fusion(bf16[16,64,1024]{1,0,2:T(8,128)(2,1)S(1)} %get-tuple-element.16, bf16[16,64,1024]{1,0,2:T(8,128)(2,1)} %get-tuple-element.24, bf16[16,64,1024]{1,0,2:T(8,128)(2,1)} %get-tuple-element.26, bf16[16,64,1024]{1,0,2:T(8,128)(2,1)} %get-tuple-element.17), kind=kOutput, calls=%fused_computation.4 | convolution fusion | flops 289406976 | bytes 16777216 | tf_op jit(solution)/shard_map/while/body/eval_jaxpr/wif,wjf->fij/dot_general | solution.py:49
  899.0 22.7 %pad_maximum_fusion = bf16[2048,64,64]{2,1,0:T(8,128)(2,1)} fusion(bf16[1024,64,64]{2,1,0:T(8,128)(2,1)} %convolution_convert_fusion, bf16[1024,64,64]{2,1,0:T(8,128)(2,1)} %convolution_convert_fusion.1), kind=kLoop, calls=%fused_computation | loop fusion | flops 8388608 | bytes 33554432 | tf_op jit(solution)/shard_map/while/body/eval_jaxpr/concatenate | solution.py:51
  921.7 35.5 %copy.47 = bf16[2048,64,64]{0,2,1:T(8,128)(2,1)} copy(bf16[2048,64,64]{2,1,0:T(8,128)(2,1)} %pad_maximum_fusion) | data formatting | bytes 33554432 | tf_op jit(solution)/shard_map/while/body/eval_jaxpr/concatenate | solution.py:51
  957.2 11.3 %multiply_bitcast_fusion = f32[1,64,64,256]{3,2,1,0:T(8,128)} fusion(bf16[2048,64,64]{0,2,1:T(8,128)(2,1)} %copy.47, bf16[1024,256]{1,0:T(8,128)(2,1)S(1)} %get-tuple-element.31, bf16[1024,256]{1,0:T(8,128)(2,1)S(1)} %get-tuple-element.30), kind=kOutput, calls=%fused_computation.24 | convolution fusion | flops 4298113024 | bytes 22020096 | tf_op jit(solution)/shard_map/while/body/eval_jaxpr/dot_general | solution.py:77
  (29 shorter events, 62.9 us)
Async XLA Ops:
  6.5 42.3 %all-gather.2.cloned.1.call-start = ((), (), s32[]{:S(2)}) async-start(), calls=%async_computation | async-start | bytes 4718592 | tf_op jit(solution)/shard_map/all_gather | solution.py:62
  7.9 327.1 %copy-start = (s32[1,2]{1,0:T(1,128)S(1)}, s32[1,2]{1,0:T(1,128)}, u32[]{:S(2)}) copy-start(s32[1,2]{1,0:T(1,128)} %param.3) | copy-start | bytes 28
  53.7 277.8 %collective-permute-start = (bf16[2,16,64,1024]{3,2,1,0:T(8,128)(2,1)}, bf16[2,16,64,1024]{3,2,1,0:T(8,128)(2,1)}, u32[]{:S(2)}, u32[]{:S(2)}) collective-permute-start(bf16[2,16,64,1024]{3,2,1,0:T(8,128)(2,1)} %copy.32), channel_id=1, source_target_pairs={{232,0},{240,8},{248,16},{0,24},{8,32},{16,40},{24,48},{32,56},{40... | collective-permute-start | bytes 12582920 | tf_op jit(solution)/shard_map/ppermute | solution.py:17
  57.3 454.4 %collective-permute-start.1 = (bf16[2,16,64,1024]{3,2,1,0:T(8,128)(2,1)}, bf16[2,16,64,1024]{3,2,1,0:T(8,128)(2,1)}, u32[]{:S(2)}, u32[]{:S(2)}) collective-permute-start(bf16[2,16,64,1024]{3,2,1,0:T(8,128)(2,1)} %copy.32), channel_id=1, source_target_pairs={{240,0},{248,8},{0,16},{8,24},{16,32},{24,40},{32,48},{40,56},{48,... | collective-permute-start | bytes 12582920 | tf_op jit(solution)/shard_map/ppermute | solution.py:17
  60.1 541.3 %collective-permute-start.2 = (bf16[2,16,64,1024]{3,2,1,0:T(8,128)(2,1)}, bf16[2,16,64,1024]{3,2,1,0:T(8,128)(2,1)}, u32[]{:S(2)}, u32[]{:S(2)}) collective-permute-start(bf16[2,16,64,1024]{3,2,1,0:T(8,128)(2,1)} %copy.32), channel_id=1, source_target_pairs={{248,0},{0,8},{8,16},{16,24},{24,32},{32,40},{40,48},{48,56},{56,6... | collective-permute-start | bytes 12582920 | tf_op jit(solution)/shard_map/ppermute | solution.py:17
  60.8 551.5 %collective-permute-start.3 = (bf16[2,16,64,1024]{3,2,1,0:T(8,128)(2,1)}, bf16[2,16,64,1024]{3,2,1,0:T(8,128)(2,1)}, u32[]{:S(2)}, u32[]{:S(2)}) collective-permute-start(bf16[2,16,64,1024]{3,2,1,0:T(8,128)(2,1)} %copy.32), channel_id=1, source_target_pairs={{8,0},{16,8},{24,16},{32,24},{40,32},{48,40},{56,48},{64,56},{72,6... | collective-permute-start | bytes 12582920 | tf_op jit(solution)/shard_map/ppermute | solution.py:17
  64.3 559.0 %collective-permute-start.4 = (bf16[2,16,64,1024]{3,2,1,0:T(8,128)(2,1)}, bf16[2,16,64,1024]{3,2,1,0:T(8,128)(2,1)}, u32[]{:S(2)}, u32[]{:S(2)}) collective-permute-start(bf16[2,16,64,1024]{3,2,1,0:T(8,128)(2,1)} %copy.32), channel_id=1, source_target_pairs={{16,0},{24,8},{32,16},{40,24},{48,32},{56,40},{64,48},{72,56},{80,... | collective-permute-start | bytes 12582920 | tf_op jit(solution)/shard_map/ppermute | solution.py:17
  331.5 454.1 %collective-permute-start.5 = (bf16[2,16,64,1024]{3,2,1,0:T(8,128)(2,1)}, bf16[2,16,64,1024]{3,2,1,0:T(8,128)(2,1)}, u32[]{:S(2)}, u32[]{:S(2)}) collective-permute-start(bf16[2,16,64,1024]{3,2,1,0:T(8,128)(2,1)} %copy.32), channel_id=1, source_target_pairs={{24,0},{32,8},{40,16},{48,24},{56,32},{64,40},{72,48},{80,56},{88,... | collective-permute-start | bytes 12582920 | tf_op jit(solution)/shard_map/ppermute | solution.py:17
  511.7 325.2 %collective-permute-start.6 = (bf16[2,16,64,1024]{3,2,1,0:T(8,128)(2,1)}, bf16[2,16,64,1024]{3,2,1,0:T(8,128)(2,1)}, u32[]{:S(2)}, u32[]{:S(2)}) collective-permute-start(bf16[2,16,64,1024]{3,2,1,0:T(8,128)(2,1)} %copy.32), channel_id=1, source_target_pairs={{32,0},{40,8},{48,16},{56,24},{64,32},{72,40},{80,48},{88,56},{96,... | collective-permute-start | bytes 12582920 | tf_op jit(solution)/shard_map/ppermute | solution.py:17
Sparse Core Ops, SparseCore 0:
  11.2 37.5 all-gather.1
where the time goes:
time: 986 us; the launch traced here: 976 us
  waiting for transfers between devices  662 us (67%)
  local copies, waits for them, and re-layouts  202 us (20%)
  matrix products  41.7 us (4%)
  other arithmetic  34.5 us (3%)
  starting transfers between devices  19.5 us (2%)
  between operations  14.9 us (2%)
    ppermute x7, waiting for transfers between devices, shifted(): return lax.ppermute(block, axis, route)  625 us
    ppermute x7, local copies, waits for them, and re-layouts, shifted(): return lax.ppermute(block, axis, route)  76.5 us
    unnamed x9, local copies, waits for them, and re-layouts  56.3 us
    all_gather x1, waiting for transfers between devices, per_device(): gathered = lax.all_gather(whitened, 'win', axis=1, tiled=True)  37.7 us
    concatenate x1, local copies, waits for them, and re-layouts, cross_spectrum(): jnp.concatenate([real_sum.astype(jnp.bfloat16), imag_sum.astype(jnp.bfloa...  35.5 us
    concatenate x1, other arithmetic, cross_spectrum(): jnp.concatenate([real_sum.astype(jnp.bfloat16), imag_sum.astype(jnp.bfloa...  22.7 us
  transfers between devices with their start and end apart: 8, of which 5 were waited for; matrix products, arithmetic and copies ran while one was open for 14% of the time, Pallas kernels for 0%

commit v1 on v0

--- a/solution.py
+++ b/solution.py
@@ -59,7 +59,9 @@
     block_count = lax.axis_size("chan")
     reach = pair_blocks.shape[0] * lax.axis_size("win") // 2
     offsets = range(1 - reach, reach + 1)
-    gathered = lax.all_gather(whitened, "win", axis=1, tiled=True)
+    gathered = jnp.concatenate(
+        lax.all_to_all(jnp.stack([whitened] * lax.axis_size("win")), "win", 0, 0), axis=1
+    )
     nearby = jnp.stack(
         [gathered if offset == 0 else shifted(gathered, "chan", -offset) for offset in offsets]
     )

time: 986 us -> 1020 us (1.034)
  the two profiles are of different devices: /device:TPU:6 before, /device:TPU:70 now
where the time goes in v1:
time: 1020 us; the launch traced here: 1010 us
  waiting for transfers between devices  645 us (63%)
  local copies, waits for them, and re-layouts  211 us (21%)
  blocking collectives  54.6 us (5%)
  matrix products  41.8 us (4%)
  other arithmetic  34.6 us (3%)
  starting transfers between devices  16.4 us (2%)
    ppermute x7, waiting for transfers between devices, shifted(): return lax.ppermute(block, axis, route)  645 us
    ppermute x7, local copies, waits for them, and re-layouts, shifted(): return lax.ppermute(block, axis, route)  76.6 us
    unnamed x11, local copies, waits for them, and re-layouts  58.2 us
    all_to_all x1, blocking collectives, per_device(): lax.all_to_all(jnp.stack([whitened] * lax.axis_size('win')), 'win', 0, 0)  54.6 us
    concatenate x1, local copies, waits for them, and re-layouts, cross_spectrum(): jnp.concatenate([real_sum.astype(jnp.bfloat16), imag_sum.astype(jnp.bfloa...  35.4 us
    concatenate x1, other arithmetic, cross_spectrum(): jnp.concatenate([real_sum.astype(jnp.bfloat16), imag_sum.astype(jnp.bfloa...  22.7 us
    reshape x1, local copies, waits for them, and re-layouts, per_device(): jnp.concatenate(lax.all_to_all(jnp.stack([whitened] * lax.axis_size('win'...  20.6 us
  transfers between devices with their start and end apart: 7, of which 3 were waited for; matrix products, arithmetic and copies ran while one was open for 15% of the time, Pallas kernels for 0%

profile of v1, /device:TPU:70, one launch (start us, length us, event | category | flops | bytes accessed | tf_op | source)
XLA Modules:
  0.0 1005.6 jit_solution(7392559595535675110)
XLA Ops:
  4.2 54.6 %all_to_all.5 = bf16[8,2,2,64,1024]{4,3,2,1,0:T(8,128)(2,1)S(1)} all-to-all(bf16[8,2,2,64,1024]{4,3,2,1,0:T(8,128)(2,1)S(1)} %stack.41), channel_id=1, replica_groups=mesh['chan'=32,'win'=8] {'win'}, dimensions={0} | all-to-all | bytes 8388608 | tf_op jit(solution)/shard_map/all_to_all | solution.py:63
  75.2 263.5 %collective-permute-done = bf16[2,16,64,1024]{3,2,1,0:T(8,128)(2,1)} collective-permute-done((bf16[2,16,64,1024]{3,2,1,0:T(8,128)(2,1)}, bf16[2,16,64,1024]{3,2,1,0:T(8,128)(2,1)}, u32[]{:S(2)}, u32[]{:S(2)}) %collective-permute-start) | collective-permute-done | bytes 4194336 | tf_op jit(solution)/shard_map/ppermute | solution.py:17
  348.9 20.6 %copy.30 = bf16[2,8,2,64,1024]{3,2,1,4,0:T(2,128)(2,1)} copy(bf16[2,8,2,64,1024]{4,3,2,0,1:T(8,128)(2,1)} %bitcast.47) | data formatting | bytes 8388608 | tf_op jit(solution)/shard_map/reshape | solution.py:62
  369.5 10.9 %copy.27 = bf16[2,16,64,1024]{2,1,3,0:T(8,128)(2,1)} copy(bf16[2,16,64,1024]{3,2,1,0:T(8,128)(2,1)} %collective-permute-done) | data formatting | bytes 8388608 | tf_op jit(solution)/shard_map/ppermute | solution.py:17
  380.4 140.5 %collective-permute-done.1 = bf16[2,16,64,1024]{3,2,1,0:T(8,128)(2,1)} collective-permute-done((bf16[2,16,64,1024]{3,2,1,0:T(8,128)(2,1)}, bf16[2,16,64,1024]{3,2,1,0:T(8,128)(2,1)}, u32[]{:S(2)}, u32[]{:S(2)}) %collective-permute-start.1) | collective-permute-done | bytes 4194336 | tf_op jit(solution)/shard_map/ppermute | solution.py:17
  521.4 10.9 %copy.28 = bf16[2,16,64,1024]{2,1,3,0:T(8,128)(2,1)} copy(bf16[2,16,64,1024]{3,2,1,0:T(8,128)(2,1)} %collective-permute-done.1) | data formatting | bytes 8388608 | tf_op jit(solution)/shard_map/ppermute | solution.py:17
  532.3 8.0 bitcast_dynamic-update-slice_fusion.6
  540.3 8.1 bitcast_dynamic-update-slice_fusion.5
  548.4 241.3 %collective-permute-done.2 = bf16[2,16,64,1024]{3,2,1,0:T(8,128)(2,1)} collective-permute-done((bf16[2,16,64,1024]{3,2,1,0:T(8,128)(2,1)}, bf16[2,16,64,1024]{3,2,1,0:T(8,128)(2,1)}, u32[]{:S(2)}, u32[]{:S(2)}) %collective-permute-start.2) | collective-permute-done | bytes 4194336 | tf_op jit(solution)/shard_map/ppermute | solution.py:17
  789.7 10.9 %copy.29 = bf16[2,16,64,1024]{2,1,3,0:T(8,128)(2,1)} copy(bf16[2,16,64,1024]{3,2,1,0:T(8,128)(2,1)} %collective-permute-done.2) | data formatting | bytes 8388608 | tf_op jit(solution)/shard_map/ppermute | solution.py:17
  800.6 10.9 %copy.31 = bf16[2,16,64,1024]{2,1,3,0:T(8,128)(2,1)} copy(bf16[2,16,64,1024]{3,2,1,0:T(8,128)(2,1)} %collective-permute-done.3) | data formatting | bytes 8388608 | tf_op jit(solution)/shard_map/ppermute | solution.py:17
  811.5 10.9 %copy.32 = bf16[2,16,64,1024]{2,1,3,0:T(8,128)(2,1)} copy(bf16[2,16,64,1024]{3,2,1,0:T(8,128)(2,1)} %collective-permute-done.4) | data formatting | bytes 8388608 | tf_op jit(solution)/shard_map/ppermute | solution.py:17
  822.4 11.1 %copy.33 = bf16[2,16,64,1024]{2,1,3,0:T(8,128)(2,1)} copy(bf16[2,16,64,1024]{3,2,1,0:T(8,128)(2,1)} %collective-permute-done.5) | data formatting | bytes 8388608 | tf_op jit(solution)/shard_map/ppermute | solution.py:17
  833.5 8.0 bitcast_dynamic-update-slice_fusion.4
  841.6 8.0 constant_dynamic-update-slice_fusion
  865.7 8.0 bitcast_dynamic-update-slice_fusion.1
  873.7 11.0 %copy.34 = bf16[2,16,64,1024]{2,1,3,0:T(8,128)(2,1)} copy(bf16[2,16,64,1024]{3,2,1,0:T(8,128)(2,1)} %collective-permute-done.6) | data formatting | bytes 8388608 | tf_op jit(solution)/shard_map/ppermute | solution.py:17
  884.7 8.0 bitcast_dynamic-update-slice_fusion
  897.7 8.8 dynamic-slice_bitcast_fusion.3
  906.5 15.7 %convolution_convert_fusion = bf16[1024,64,64]{2,1,0:T(8,128)(2,1)} fusion(bf16[16,64,1024]{1,0,2:T(8,128)(2,1)} %get-tuple-element.24, bf16[16,64,1024]{1,0,2:T(8,128)(2,1)} %get-tuple-element.15, bf16[16,64,1024]{1,0,2:T(8,128)(2,1)} %get-tuple-element.26, bf16[16,64,1024]{1,0,2:T(8,128)(2,1)} %get-tuple-element.17), kind=kOutput, calls=%fused_computation.3 | convolution fusion | flops 289406976 | bytes 16777216 | tf_op jit(solution)/shard_map/while/body/eval_jaxpr/wif,wjf->fij/dot_general | solution.py:50
  922.2 13.8 %convolution_convert_fusion.1 = bf16[1024,64,64]{2,1,0:T(8,128)(2,1)} fusion(bf16[16,64,1024]{1,0,2:T(8,128)(2,1)S(1)} %get-tuple-element.16, bf16[16,64,1024]{1,0,2:T(8,128)(2,1)} %get-tuple-element.24, bf16[16,64,1024]{1,0,2:T(8,128)(2,1)} %get-tuple-element.26, bf16[16,64,1024]{1,0,2:T(8,128)(2,1)} %get-tuple-element.17), kind=kOutput, calls=%fused_computation.4 | convolution fusion | flops 289406976 | bytes 16777216 | tf_op jit(solution)/shard_map/while/body/eval_jaxpr/wif,wjf->fij/dot_general | solution.py:49
  935.9 22.7 %pad_maximum_fusion = bf16[2048,64,64]{2,1,0:T(8,128)(2,1)} fusion(bf16[1024,64,64]{2,1,0:T(8,128)(2,1)} %convolution_convert_fusion, bf16[1024,64,64]{2,1,0:T(8,128)(2,1)} %convolution_convert_fusion.1), kind=kLoop, calls=%fused_computation | loop fusion | flops 8388608 | bytes 33554432 | tf_op jit(solution)/shard_map/while/body/eval_jaxpr/concatenate | solution.py:51
  958.7 35.4 %copy.35 = bf16[2048,64,64]{0,2,1:T(8,128)(2,1)} copy(bf16[2048,64,64]{2,1,0:T(8,128)(2,1)} %pad_maximum_fusion) | data formatting | bytes 33554432 | tf_op jit(solution)/shard_map/while/body/eval_jaxpr/concatenate | solution.py:51
  994.1 11.3 %multiply_bitcast_fusion = f32[1,64,64,256]{3,2,1,0:T(8,128)} fusion(bf16[2048,64,64]{0,2,1:T(8,128)(2,1)} %copy.35, bf16[1024,256]{1,0:T(8,128)(2,1)S(1)} %get-tuple-element.31, bf16[1024,256]{1,0:T(8,128)(2,1)S(1)} %get-tuple-element.30), kind=kOutput, calls=%fused_computation.23 | convolution fusion | flops 4298113024 | bytes 22020096 | tf_op jit(solution)/shard_map/while/body/eval_jaxpr/dot_general | solution.py:79
  (29 shorter events, 50.9 us)
Async XLA Ops:
  4.2 338.5 %copy-start.1 = (s32[1,2]{1,0:T(1,128)S(1)}, s32[1,2]{1,0:T(1,128)}, u32[]{:S(2)}) copy-start(s32[1,2]{1,0:T(1,128)} %param.3) | copy-start | bytes 28
  58.8 2.0 copy-start
  63.2 275.5 %collective-permute-start = (bf16[2,16,64,1024]{3,2,1,0:T(8,128)(2,1)}, bf16[2,16,64,1024]{3,2,1,0:T(8,128)(2,1)}, u32[]{:S(2)}, u32[]{:S(2)}) collective-permute-start(bf16[2,16,64,1024]{3,2,1,0:T(8,128)(2,1)} %bitcast.3), channel_id=1, source_target_pairs={{232,0},{240,8},{248,16},{0,24},{8,32},{16,40},{24,48},{32,56},{40... | collective-permute-start | bytes 12582920 | tf_op jit(solution)/shard_map/ppermute | solution.py:17
  68.2 452.7 %collective-permute-start.1 = (bf16[2,16,64,1024]{3,2,1,0:T(8,128)(2,1)}, bf16[2,16,64,1024]{3,2,1,0:T(8,128)(2,1)}, u32[]{:S(2)}, u32[]{:S(2)}) collective-permute-start(bf16[2,16,64,1024]{3,2,1,0:T(8,128)(2,1)} %bitcast.3), channel_id=1, source_target_pairs={{240,0},{248,8},{0,16},{8,24},{16,32},{24,40},{32,48},{40,56},{48,... | collective-permute-start | bytes 12582920 | tf_op jit(solution)/shard_map/ppermute | solution.py:17
  69.6 720.1 %collective-permute-start.2 = (bf16[2,16,64,1024]{3,2,1,0:T(8,128)(2,1)}, bf16[2,16,64,1024]{3,2,1,0:T(8,128)(2,1)}, u32[]{:S(2)}, u32[]{:S(2)}) collective-permute-start(bf16[2,16,64,1024]{3,2,1,0:T(8,128)(2,1)} %bitcast.3), channel_id=1, source_target_pairs={{248,0},{0,8},{8,16},{16,24},{24,32},{32,40},{40,48},{48,56},{56,6... | collective-permute-start | bytes 12582920 | tf_op jit(solution)/shard_map/ppermute | solution.py:17
  69.6 730.9 %collective-permute-start.3 = (bf16[2,16,64,1024]{3,2,1,0:T(8,128)(2,1)}, bf16[2,16,64,1024]{3,2,1,0:T(8,128)(2,1)}, u32[]{:S(2)}, u32[]{:S(2)}) collective-permute-start(bf16[2,16,64,1024]{3,2,1,0:T(8,128)(2,1)} %bitcast.3), channel_id=1, source_target_pairs={{8,0},{16,8},{24,16},{32,24},{40,32},{48,40},{56,48},{64,56},{72,6... | collective-permute-start | bytes 12582920 | tf_op jit(solution)/shard_map/ppermute | solution.py:17
  71.7 739.9 %collective-permute-start.4 = (bf16[2,16,64,1024]{3,2,1,0:T(8,128)(2,1)}, bf16[2,16,64,1024]{3,2,1,0:T(8,128)(2,1)}, u32[]{:S(2)}, u32[]{:S(2)}) collective-permute-start(bf16[2,16,64,1024]{3,2,1,0:T(8,128)(2,1)} %bitcast.3), channel_id=1, source_target_pairs={{16,0},{24,8},{32,16},{40,24},{48,32},{56,40},{64,48},{72,56},{80,... | collective-permute-start | bytes 12582920 | tf_op jit(solution)/shard_map/ppermute | solution.py:17
  338.7 483.7 %collective-permute-start.5 = (bf16[2,16,64,1024]{3,2,1,0:T(8,128)(2,1)}, bf16[2,16,64,1024]{3,2,1,0:T(8,128)(2,1)}, u32[]{:S(2)}, u32[]{:S(2)}) collective-permute-start(bf16[2,16,64,1024]{3,2,1,0:T(8,128)(2,1)} %bitcast.3), channel_id=1, source_target_pairs={{24,0},{32,8},{40,16},{48,24},{56,32},{64,40},{72,48},{80,56},{88,... | collective-permute-start | bytes 12582920 | tf_op jit(solution)/shard_map/ppermute | solution.py:17
  520.9 352.8 %collective-permute-start.6 = (bf16[2,16,64,1024]{3,2,1,0:T(8,128)(2,1)}, bf16[2,16,64,1024]{3,2,1,0:T(8,128)(2,1)}, u32[]{:S(2)}, u32[]{:S(2)}) collective-permute-start(bf16[2,16,64,1024]{3,2,1,0:T(8,128)(2,1)} %bitcast.3), channel_id=1, source_target_pairs={{32,0},{40,8},{48,16},{56,24},{64,32},{72,40},{80,48},{88,56},{96,... | collective-permute-start | bytes 12582920 | tf_op jit(solution)/shard_map/ppermute | solution.py:17
